TPU v7x, 128 devices: a whole 4x4x4 slice. The times are simulated.
128 devices in a mesh: req: 64 (over y, z, x), tp: 2 (over core).
Axes of the slice: x: 4, y: 4, z: 4, core: 2. Of those that a mesh axis runs over, the one named last changes fastest.
Arguments:
- tokens: bfloat16 [12288, 1536], P('req', 'tp'), may hold values from -6 to 6
- video_lengths: int32 [5], replicated, may hold values from 1 to 7680, 12288 in all
- timestep: int32 [1], replicated, may hold values from 1 to 1000
- time_weight: float32 [256, 4608], replicated, may hold values from -0.375 to 0.375
- block_mod: float32 [3, 1536], replicated, may hold values from -3 to 3
- w_query: bfloat16 [1536, 1536], P(None, 'tp')
- w_key: bfloat16 [1536, 1536], P(None, 'tp')
- w_value: bfloat16 [1536, 1536], P(None, 'tp'), may hold values from -0.15625 to 0.15625
- w_out: bfloat16 [1536, 1536], P('tp'), may hold values from -0.15625 to 0.15625
Outputs:
- velocity: bfloat16 [12288, 1536], P('req', 'tp')
- stepped: bfloat16 [12288, 1536], P('req', 'tp')
Inputs may be any that keep to these rules, and one draw needn't show every extreme that they name: `video_lengths`: the videos' lengths in packing order; they sum to 12288 and the longest has exactly 7680 tokens.
All inputs are finite; a program needn't handle non-finite values.
Results may differ from a plain program's by a relative error of at most 0.017.
Values may be sent and summed in bfloat16 or wider, within the bound.
A program may use at most 256 MiB of HBM per device.

v0:
```python
import math
import jax
import jax.numpy as jnp
from jax import lax
from jax.sharding import PartitionSpec as P

HEAD_DIM = 128
STEPS = 1000


def noise_level(step_value):
    frac = step_value / STEPS
    return 5.0 * frac / (1.0 + 4.0 * frac)


def on_device(
    tokens, video_lengths, timestep, time_weight, block_mod, w_query, w_key, w_value, w_out
):
    tok_rows = tokens.shape[0]
    width = time_weight.shape[1] // 3
    full_rows = lax.all_gather(tokens, "tp", axis=1, tiled=True)
    time_value = timestep[0].astype(jnp.float32)
    sigma = noise_level(time_value)
    delta_sigma = noise_level(time_value - 1.0) - sigma
    half_freq = time_weight.shape[0] // 2
    frequency = jnp.exp(-math.log(10000.0) * jnp.arange(half_freq, dtype=jnp.float32) / half_freq)
    angle = 1000.0 * sigma * frequency
    embedding = jnp.concatenate([jnp.cos(angle), jnp.sin(angle)])
    modulation = jnp.dot(
        jax.nn.silu(embedding)[None, :],
        time_weight,
        precision=lax.Precision.HIGHEST,
        preferred_element_type=jnp.float32,
    )[0]
    modulation = modulation.reshape(3, width) + block_mod
    shift, scale, gate = (modulation[0], modulation[1], modulation[2])
    as_float = full_rows.astype(jnp.float32)
    mean = jnp.mean(as_float, axis=1, keepdims=True)
    centred = as_float - mean
    variance = jnp.mean(centred * centred, axis=1, keepdims=True)
    normed = (centred * lax.rsqrt(variance + 1e-06) * (1.0 + scale) + shift).astype(jnp.bfloat16)
    query = jnp.dot(normed, w_query, preferred_element_type=jnp.float32).astype(jnp.bfloat16)
    keys = jnp.dot(normed, w_key, preferred_element_type=jnp.float32).astype(jnp.bfloat16)
    values = jnp.dot(normed, w_value, preferred_element_type=jnp.float32).astype(jnp.bfloat16)
    heads_here = query.shape[1] // HEAD_DIM
    query_heads = query.reshape(tok_rows, heads_here, HEAD_DIM)
    start_row = lax.axis_index("req") * tok_rows
    query_index = start_row + jnp.arange(tok_rows, dtype=jnp.int32)
    video_ends = jnp.cumsum(video_lengths)
    video_starts = video_ends - video_lengths
    inside = jnp.logical_and(
        query_index[:, None] >= video_starts[None, :], query_index[:, None] < video_ends[None, :]
    )
    query_low = jnp.sum(jnp.where(inside, video_starts[None, :], 0), axis=1)
    query_high = jnp.sum(jnp.where(inside, video_ends[None, :], 0), axis=1)
    key_index = jnp.arange(tok_rows * lax.psum(1, "req"), dtype=jnp.int32)
    valid = jnp.logical_and(
        key_index[None, :] >= query_low[:, None], key_index[None, :] < query_high[:, None]
    )
    outputs = []
    for head in range(heads_here):
        cols = slice(head * HEAD_DIM, (head + 1) * HEAD_DIM)
        packed = jnp.concatenate([keys[:, cols], values[:, cols]], axis=1)
        gathered = lax.all_gather(packed, "req", axis=0, tiled=True)
        key_head = gathered[:, :HEAD_DIM]
        value_head = gathered[:, HEAD_DIM:]
        scores = jnp.dot(
            query[:, cols], key_head.T, preferred_element_type=jnp.float32
        ) / math.sqrt(HEAD_DIM)
        row_max = jnp.max(jnp.where(valid, scores, -1e30), axis=1, keepdims=True)
        probs = jnp.where(valid, jnp.exp(scores - row_max), 0.0)
        row_sum = jnp.sum(probs, axis=1, keepdims=True)
        weighted = jnp.dot(
            probs.astype(jnp.bfloat16), value_head, preferred_element_type=jnp.float32
        )
        outputs.append((weighted / row_sum).astype(jnp.bfloat16))
    attended = jnp.concatenate(outputs, axis=1)
    partial_value = jnp.dot(attended, w_out, preferred_element_type=jnp.float32)
    own_sum = lax.psum_scatter(
        partial_value.astype(jnp.bfloat16), "tp", scatter_dimension=1, tiled=True
    ).astype(jnp.float32)
    share = own_sum.shape[1]
    gate_share = lax.dynamic_slice_in_dim(gate, lax.axis_index("tp") * share, share)
    branch = gate_share[None, :] * own_sum
    velocity = branch.astype(jnp.bfloat16)
    stepped = (tokens.astype(jnp.float32) + delta_sigma * branch).astype(jnp.bfloat16)
    return (velocity, stepped)


def solution(mesh):
    return jax.shard_map(
        on_device,
        mesh=mesh,
        in_specs=(
            P("req", "tp"),
            P(),
            P(),
            P(),
            P(),
            P(None, "tp"),
            P(None, "tp"),
            P(None, "tp"),
            P("tp", None),
        ),
        out_specs=(P("req", "tp"), P("req", "tp")),
        check_vma=False,
    )
```

profile of v0, /device:TPU:1, one launch (start us, length us, event | category | flops | bytes accessed | tf_op | source)
XLA Modules:
  0.0 568.4 jit_solution(9086971898280065333)
XLA Ops:
  8.1 3.5 all_gather.21
  12.1 6.0 %copy.12 = f32[256,4608]{0,1:T(8,128)} copy(f32[256,4608]{1,0:T(8,128)} %param.12) | data formatting | bytes 9437184 | tf_op args[3]
  18.2 6.4 %fusion.172 = f32[1,3,1536]{2,0,1:T(1,128)S(1)} fusion(f32[256,1,1]{0,1,2:T(1,128)S(1)} %bitcast.27, f32[3,1536,256]{2,1,0:T(8,128)} %bitcast.24), kind=kOutput, calls=%fused_computation.133 | convolution fusion | flops 14155776 | bytes 4738048 | tf_op jit(solution)/shard_map/dot_general | solution.py:29
  24.6 2.4 convolution_convert_fusion.2
  27.0 0.7 convolution_convert_fusion.1
  27.9 0.7 pad_maximum_fusion
  28.6 0.7 pad_maximum_fusion.2
  30.1 0.6 pad_maximum_fusion.4
  30.8 0.7 pad_maximum_fusion.5
  32.7 2.4 convolution_convert_fusion.3
  35.1 67.6 %all-gather.7.cloned.1.call-done = bf16[12288,256]{1,0:T(8,128)(2,1)} async-done(((bf16[192,256]{1,0:T(8,128)(2,1)}), bf16[12288,256]{1,0:T(8,128)(2,1)}) %all-gather.7.cloned.1.call-update) | async-done | bytes 6291472 | tf_op jit(solution)/shard_map/all_gather | solution.py:64
  102.7 6.9 %convolution_multiply_fusion.5 = f32[192,12288]{1,0:T(8,128)} fusion(bf16[12288,256]{1,0:T(8,128)(2,1)} %all-gather.7.cloned.1.call-done, bf16[192,768]{1,0:T(8,128)(2,1)S(1)} %convolution_convert_fusion.3), kind=kOutput, calls=%fused_computation.5 | convolution fusion | flops 606339072 | bytes 12632064 | tf_op jit(solution)/shard_map/dot_general | solution.py:67
  109.7 67.4 %all-gather.11.cloned.1.call-done = bf16[12288,256]{1,0:T(8,128)(2,1)} async-done(((bf16[192,256]{1,0:T(8,128)(2,1)}), bf16[12288,256]{1,0:T(8,128)(2,1)}) %all-gather.11.cloned.1.call-update) | async-done | bytes 6291472 | tf_op jit(solution)/shard_map/all_gather | solution.py:64
  177.0 6.9 %convolution_multiply_fusion.3 = f32[192,12288]{1,0:T(8,128)} fusion(bf16[12288,256]{1,0:T(8,128)(2,1)} %all-gather.11.cloned.1.call-done, bf16[192,768]{1,0:T(8,128)(2,1)S(1)} %convolution_convert_fusion.3), kind=kOutput, calls=%fused_computation.3 | convolution fusion | flops 606339072 | bytes 12632064 | tf_op jit(solution)/shard_map/dot_general | solution.py:67
  184.0 67.4 %all-gather.13.cloned.1.call-done = bf16[12288,256]{1,0:T(8,128)(2,1)} async-done(((bf16[192,256]{1,0:T(8,128)(2,1)}), bf16[12288,256]{1,0:T(8,128)(2,1)}) %all-gather.13.cloned.1.call-update) | async-done | bytes 6291472 | tf_op jit(solution)/shard_map/all_gather | solution.py:64
  251.3 7.0 %convolution_multiply_fusion.2 = f32[192,12288]{1,0:T(8,128)} fusion(bf16[12288,256]{1,0:T(8,128)(2,1)} %all-gather.13.cloned.1.call-done, bf16[192,768]{1,0:T(8,128)(2,1)S(1)} %convolution_convert_fusion.3), kind=kOutput, calls=%fused_computation.2 | convolution fusion | flops 606339072 | bytes 12632064 | tf_op jit(solution)/shard_map/dot_general | solution.py:67
  258.3 67.1 %all-gather.15.cloned.1.call-done = bf16[12288,256]{1,0:T(8,128)(2,1)} async-done(((bf16[192,256]{1,0:T(8,128)(2,1)}), bf16[12288,256]{1,0:T(8,128)(2,1)}) %all-gather.15.cloned.1.call-update) | async-done | bytes 6291472 | tf_op jit(solution)/shard_map/all_gather | solution.py:64
  325.5 6.8 %convolution_multiply_fusion.1 = f32[192,12288]{1,0:T(8,128)} fusion(bf16[12288,256]{1,0:T(8,128)(2,1)} %all-gather.15.cloned.1.call-done, bf16[192,768]{1,0:T(8,128)(2,1)S(1)} %convolution_convert_fusion.3), kind=kOutput, calls=%fused_computation.1 | convolution fusion | flops 606339072 | bytes 12632064 | tf_op jit(solution)/shard_map/dot_general | solution.py:67
  332.3 67.9 %all-gather.17.cloned.1.call-done = bf16[12288,256]{1,0:T(8,128)(2,1)} async-done(((bf16[192,256]{1,0:T(8,128)(2,1)}), bf16[12288,256]{1,0:T(8,128)(2,1)}) %all-gather.17.cloned.1.call-update) | async-done | bytes 6291472 | tf_op jit(solution)/shard_map/all_gather | solution.py:64
  400.2 13.5 %select_reduce_fusion = (f32[192]{0:T(256)S(1)}, f32[192]{0:T(256)S(1)}, f32[192,12288]{1,0:T(8,128)}) fusion(s32[192]{0:T(256)S(1)} %get-tuple-element.17, s32[192]{0:T(256)S(1)} %get-tuple-element.16, f32[192,12288]{1,0:T(8,128)} %convolution_multiply_fusion.5, bf16[12288,256]{1,0:T(8,128)(2,1)} %all-gather.17.cloned.1.call-done, ...), kind=kOutput, calls=%fused_computation.7 | convolution fusion | flops 622853760 | bytes 22072832 | tf_op jit(solution)/shard_map/dot_general | solution.py:67
  413.6 60.7 %all-gather.9.cloned.1.call-done = bf16[12288,256]{1,0:T(8,128)(2,1)} async-done(((bf16[192,256]{1,0:T(8,128)(2,1)}), bf16[12288,256]{1,0:T(8,128)(2,1)}) %all-gather.9.cloned.1.call-update) | async-done | bytes 6291472 | tf_op jit(solution)/shard_map/all_gather | solution.py:64
  474.3 23.0 %fusion.11 = (f32[192]{0:T(256)S(1)}, f32[192]{0:T(256)S(1)}, f32[192]{0:T(256)S(1)}, f32[192]{0:T(256)S(1)}, f32[192]{0:T(256)S(1)}, /*index=5*/f32[192]{0:T(256)S(1)}, f32[192,12288]{1,0:T(8,128)}) fusion(f32[192,12288]{1,0:T(8,128)} %get-tuple-element.33, f32[192]{0:T(256)S(1)} %get-tuple-element.10, s32[192]{0:T(256)S(1)} %get-tuple-element.17, ...), kind=kOutput, calls=%fused_computation.31 | convolution fusion | flops 646445952 | bytes 59826688 | tf_op jit(solution)/shard_map/dot_general | solution.py:67
  497.4 13.4 %fusion.9 = (f32[192]{0:T(256)S(1)}, f32[192]{0:T(256)S(1)}, f32[192]{0:T(256)S(1)}, f32[192]{0:T(256)S(1)}) fusion(f32[192,12288]{1,0:T(8,128)S(1)} %bitcast.19, f32[192]{0:T(256)S(1)} %get-tuple-element.8, s32[192]{0:T(256)S(1)} %get-tuple-element.17, s32[192]{0:T(256)S(1)} %get-tuple-element.16, f32[192,12288]{1,0:T(8,128)} %get-tuple-element.34, ...), kind=kLoop, calls=%fused_computation.29 | loop fusion | flops 35388672 | bytes 37756416 | tf_op jit(solution)/shard_map/reduce_sum | solution.py:72
  510.9 7.7 %fusion.65 = bf16[192,768]{1,0:T(8,128)(2,1)S(1)} fusion(bf16[12288,256]{1,0:T(8,128)(2,1)} %all-gather.7.cloned.1.call-done, f32[192,12288]{1,0:T(8,128)} %convolution_multiply_fusion.5, f32[192]{0:T(256)S(1)} %get-tuple-element.11, f32[192]{0:T(256)S(1)} %get-tuple-element.9, s32[192]{0:T(256)S(1)} %get-tuple-element.17, s32[192]{0:T(256)S(1)} %get-tuple-element.16), kind=kOutput, calls=%fused_computation.77 | convolution fusion | flops 618184704 | bytes 12635136 | tf_op jit(solution)/shard_map/dot_general | solution.py:73
  518.6 7.8 %fusion.80 = bf16[192,768]{1,0:T(8,128)(2,1)S(1)} fusion(bf16[192,768]{1,0:T(8,128)(2,1)S(1)} %fusion.65, bf16[12288,256]{1,0:T(8,128)(2,1)} %all-gather.9.cloned.1.call-done, f32[192,12288]{1,0:T(8,128)} %get-tuple-element.34, f32[192]{0:T(256)S(1)} %get-tuple-element.5, f32[192]{0:T(256)S(1)} %get-tuple-element.13, s32[192]{0:T(256)S(1)} %get-tuple-element.17, ...), kind=kOutput, calls=%fused_computation.80 | convolution fusion | flops 618184704 | bytes 12636160 | tf_op jit(solution)/shard_map/dot_general | solution.py:73
  526.4 5.2 fusion.95
  531.7 5.4 fusion.110
  537.1 3.1 fusion.125
  540.3 6.8 %fusion.140 = bf16[192,768]{1,0:T(8,128)(2,1)S(1)} fusion(bf16[192,768]{1,0:T(8,128)(2,1)S(1)} %fusion.125, bf16[12288,256]{1,0:T(8,128)(2,1)S(1)} %bitcast.30, f32[192,12288]{1,0:T(8,128)} %get-tuple-element.33, f32[192]{0:T(256)S(1)} %get-tuple-element.10, f32[192]{0:T(256)S(1)} %get-tuple-element.4, s32[192]{0:T(256)S(1)} %get-tuple-element.17, ...), kind=kOutput, calls=%fused_computation.92 | convolution fusion | flops 618184704 | bytes 12636160 | tf_op jit(solution)/shard_map/dot_general | solution.py:73
  547.1 1.4 convolution_convert_fusion
  548.7 10.8 %reduce-scatter.2.cloned.1.call-done = bf16[192,768]{1,0:T(8,128)(2,1)} async-done(((bf16[192,1536]{1,0:T(8,128)(2,1)}), bf16[192,768]{1,0:T(8,128)(2,1)}) %reduce-scatter.2.cloned.1.call-update) | async-done | bytes 294928 | tf_op jit(solution)/shard_map/reduce_scatter | solution.py:79
  559.5 1.9 add_convert_fusion
  (72 shorter events, 3.0 us)
Async XLA Ops:
  7.2 540.0 %copy-start = (bf16[768,1536]{1,0:T(8,128)(2,1)S(1)}, bf16[768,1536]{1,0:T(8,128)(2,1)}, u32[]{:S(2)}) copy-start(bf16[768,1536]{1,0:T(8,128)(2,1)} %param.17) | copy-start | bytes 7077892
  7.2 95.6 %all-gather.7.cloned.1.call-start = ((), (), s32[]{:S(2)}) async-start(), calls=%async_computation.1 | async-start | bytes 6389760 | tf_op jit(solution)/shard_map/all_gather | solution.py:64
  12.1 12.4 %copy-start.2 = (f32[3,1536]{1,0:T(4,128)S(1)}, f32[3,1536]{1,0:T(4,128)}, u32[]{:S(2)}) copy-start(f32[3,1536]{1,0:T(4,128)} %param.13) | copy-start | bytes 55300
  18.1 8.9 %copy-start.3 = (bf16[1536,768]{1,0:T(8,128)(2,1)S(1)}, bf16[1536,768]{1,0:T(8,128)(2,1)}, u32[]{:S(2)}) copy-start(bf16[1536,768]{1,0:T(8,128)(2,1)} %param.16) | copy-start | bytes 7077892
  24.5 7.9 %copy-start.4 = (s32[5]{0:T(128)S(1)}, s32[5]{0:T(128)}, u32[]{:S(2)}) copy-start(s32[5]{0:T(128)} %param.10) | copy-start | bytes 64
  28.6 148.5 %all-gather.11.cloned.1.call-start = ((), (), s32[]{:S(2)}) async-start(), calls=%async_computation.3 | async-start | bytes 6389760 | tf_op jit(solution)/shard_map/all_gather | solution.py:64
  29.3 222.0 %all-gather.13.cloned.1.call-start = ((), (), s32[]{:S(2)}) async-start(), calls=%async_computation.4 | async-start | bytes 6389760 | tf_op jit(solution)/shard_map/all_gather | solution.py:64
  30.1 295.4 %all-gather.15.cloned.1.call-start = ((), (), s32[]{:S(2)}) async-start(), calls=%async_computation.5 | async-start | bytes 6389760 | tf_op jit(solution)/shard_map/all_gather | solution.py:64
  30.8 369.4 %all-gather.17.cloned.1.call-start = ((), (), s32[]{:S(2)}) async-start(), calls=%async_computation.6 | async-start | bytes 6389760 | tf_op jit(solution)/shard_map/all_gather | solution.py:64
  31.5 442.8 %all-gather.9.cloned.1.call-start = ((), (), s32[]{:S(2)}) async-start(), calls=%async_computation.2 | async-start | bytes 6389760 | tf_op jit(solution)/shard_map/all_gather | solution.py:64
  32.2 527.3 %reduce-scatter.2.cloned.1.call-start = ((), (), s32[]{:S(2)}) async-start(), calls=%async_computation.7 | async-start | bytes 884736 | tf_op jit(solution)/shard_map/reduce_scatter | solution.py:79
  474.3 23.0 %slice-start = ((s8[9437184]{0:T(1024)(128)(4,1)}), s8[4194304]{0:T(1024)(128)(4,1)S(1)}, s32[]{:S(2)}) async-start(s8[9437184]{0:T(1024)(128)(4,1)} %bitcast.18), calls=%async_computation.8 | async-start | bytes 8388608
  474.3 23.0 %slice-start.1 = ((s8[9437184]{0:T(1024)(128)(4,1)}), s8[4194304]{0:T(1024)(128)(4,1)S(1)}, s32[]{:S(2)}) async-start(s8[9437184]{0:T(1024)(128)(4,1)} %bitcast.18), calls=%async_computation.9 | async-start | bytes 8388608
  474.3 23.0 %slice-start.2 = ((s8[9437184]{0:T(1024)(128)(4,1)}), s8[1048576]{0:T(1024)(128)(4,1)S(1)}, s32[]{:S(2)}) async-start(s8[9437184]{0:T(1024)(128)(4,1)} %bitcast.18), calls=%async_computation.10 | async-start | bytes 2097152
  510.8 15.6 %slice-start.6 = ((s8[9437184]{0:T(1024)(128)(4,1)}), s8[4194304]{0:T(1024)(128)(4,1)S(1)}, s32[]{:S(2)}) async-start(s8[9437184]{0:T(1024)(128)(4,1)} %bitcast.22), calls=%async_computation.14 | async-start | bytes 8388608
  510.8 15.6 %slice-start.7 = ((s8[9437184]{0:T(1024)(128)(4,1)}), s8[4194304]{0:T(1024)(128)(4,1)S(1)}, s32[]{:S(2)}) async-start(s8[9437184]{0:T(1024)(128)(4,1)} %bitcast.22), calls=%async_computation.15 | async-start | bytes 8388608
  518.6 7.8 %slice-start.8 = ((s8[9437184]{0:T(1024)(128)(4,1)}), s8[1048576]{0:T(1024)(128)(4,1)S(1)}, s32[]{:S(2)}) async-start(s8[9437184]{0:T(1024)(128)(4,1)} %bitcast.22), calls=%async_computation.16 | async-start | bytes 2097152
  518.6 13.1 %slice-start.3 = ((s8[9437184]{0:T(1024)(128)(4,1)}), s8[4194304]{0:T(1024)(128)(4,1)S(1)}, s32[]{:S(2)}) async-start(s8[9437184]{0:T(1024)(128)(4,1)} %bitcast.20), calls=%async_computation.11 | async-start | bytes 8388608
  518.6 13.1 %slice-start.4 = ((s8[9437184]{0:T(1024)(128)(4,1)}), s8[4194304]{0:T(1024)(128)(4,1)S(1)}, s32[]{:S(2)}) async-start(s8[9437184]{0:T(1024)(128)(4,1)} %bitcast.20), calls=%async_computation.12 | async-start | bytes 8388608
  526.4 5.3 slice-start.5
  526.4 10.7 %slice-start.9 = ((s8[6291456]{0:T(1024)(128)(4,1)}), s8[2097152]{0:T(1024)(128)(4,1)S(1)}, s32[]{:S(2)}) async-start(s8[6291456]{0:T(1024)(128)(4,1)} %bitcast.25), calls=%async_computation.17 | async-start | bytes 4194304
  531.7 5.4 slice-start.10
  531.7 8.5 %slice-start.11 = ((s8[6291456]{0:T(1024)(128)(4,1)}), s8[2097152]{0:T(1024)(128)(4,1)S(1)}, s32[]{:S(2)}) async-start(s8[6291456]{0:T(1024)(128)(4,1)} %bitcast.29), calls=%async_computation.19 | async-start | bytes 4194304
  537.1 3.1 slice-start.12
  540.3 19.2 %copy-start.1 = (bf16[192,768]{1,0:T(8,128)(2,1)S(1)}, bf16[192,768]{1,0:T(8,128)(2,1)}, u32[]{:S(2)}) copy-start(bf16[192,768]{1,0:T(8,128)(2,1)} %param.9) | copy-start | bytes 884740
Sparse Core Ops, SparseCore 0:
  28.7 74.0 all-gather.6
  105.6 71.4 all-gather.10
  179.9 71.4 all-gather.12
  254.0 71.4 all-gather.14
  328.7 71.4 all-gather.16
  402.9 71.4 all-gather.8
  548.7 10.7 reduce-scatter.1
where the time goes:
time: 574 us; the launch traced here: 568 us
  waiting for transfers between devices  409 us (71%)
  matrix products  114 us (20%)
  other arithmetic  20.1 us (4%)
  between operations  15.6 us (3%)
  local copies, waits for them, and re-layouts  6.26 us (1%)
    all_gather x6, waiting for transfers between devices, on_device(): gathered = lax.all_gather(packed, 'req', axis=0, tiled=True)  398 us
    dot_general x6, matrix products, on_device(): jnp.dot(query[:, cols], key_head.T, preferred_element_type=jnp.float32)  64.1 us
    dot_general x6, matrix products, on_device(): jnp.dot(probs.astype(jnp.bfloat16), value_head, preferred_element_type=jn...  36 us
    reduce_sum x1, other arithmetic, on_device(): row_sum = jnp.sum(probs, axis=1, keepdims=True)  13.4 us
  transfers between devices with their start and end apart: 7, of which 7 were waited for; matrix products, arithmetic and copies ran while one was open for 8% of the time, Pallas kernels for 0%

commit v1 on v0

--- a/solution.py
+++ b/solution.py
@@ -61,7 +61,9 @@
     for head in range(heads_here):
         cols = slice(head * HEAD_DIM, (head + 1) * HEAD_DIM)
         packed = jnp.concatenate([keys[:, cols], values[:, cols]], axis=1)
-        gathered = lax.all_gather(packed, "req", axis=0, tiled=True)
+        gathered = jnp.concatenate(
+            lax.all_to_all(jnp.stack([packed] * lax.axis_size("req")), "req", 0, 0), axis=0
+        )
         key_head = gathered[:, :HEAD_DIM]
         value_head = gathered[:, HEAD_DIM:]
         scores = jnp.dot(

time: 574 us -> 685 us (1.19)
  starting transfers between devices: 0.47 us -> 70.3 us
  local copies, waits for them, and re-layouts: 6.26 us -> 32.3 us
  waiting for transfers between devices: 409 us -> 428 us
    all_to_all x0 -> x6, waiting for transfers between devices: none -> 409 us  [on_device(): lax.all_to_all(jnp.stack([packed] * lax.axis_size('req')), 'req', 0, 0)]
    all_gather x6 -> x0, waiting for transfers between devices: 398 us -> none  [on_device(): gathered = lax.all_gather(packed, 'req', axis=0, tiled=True)]
    all_to_all x0 -> x6, starting transfers between devices: none -> 70.3 us  [on_device(): lax.all_to_all(jnp.stack([packed] * lax.axis_size('req')), 'req', 0, 0)]
    another operation x0 -> x6, local copies, waits for them, and re-layouts: none -> 20.4 us  [on_device(): jnp.stack([packed] * lax.axis_size('req'))]
    reduce_scatter x1, waiting for transfers between devices: 10.8 us -> 19.1 us  [on_device(): lax.psum_scatter(partial_value.astype(jnp.bfloat16), 'tp', scatter_dimens...]
  transfers between devices with their start and end apart: 7 -> 7, of which waited for: 7 -> 7; matrix products, arithmetic and copies ran while one was open for 8% -> 6% of each run, Pallas kernels for 0% -> 0%
where the time goes in v1:
time: 685 us; the launch traced here: 676 us
  waiting for transfers between devices  428 us (62%)
  matrix products  111 us (16%)
  starting transfers between devices  70.3 us (10%)
  local copies, waits for them, and re-layouts  32.3 us (5%)
  between operations  15.5 us (2%)
  other arithmetic  15 us (2%)
    all_to_all x6, waiting for transfers between devices, on_device(): lax.all_to_all(jnp.stack([packed] * lax.axis_size('req')), 'req', 0, 0)  409 us
    all_to_all x6, starting transfers between devices, on_device(): lax.all_to_all(jnp.stack([packed] * lax.axis_size('req')), 'req', 0, 0)  70.3 us
    dot_general x6, matrix products, on_device(): jnp.dot(query[:, cols], key_head.T, preferred_element_type=jnp.float32)  57.4 us
    dot_general x6, matrix products, on_device(): jnp.dot(probs.astype(jnp.bfloat16), value_head, preferred_element_type=jn...  40.7 us
    another operation x6, local copies, waits for them, and re-layouts, on_device(): jnp.stack([packed] * lax.axis_size('req'))  20.4 us
    reduce_scatter x1, waiting for transfers between devices, on_device(): lax.psum_scatter(partial_value.astype(jnp.bfloat16), 'tp', scatter_dimens...  19.1 us
  transfers between devices with their start and end apart: 7, of which 7 were waited for; matrix products, arithmetic and copies ran while one was open for 6% of the time, Pallas kernels for 0%

profile of v1, /device:TPU:1, one launch (start us, length us, event | category | flops | bytes accessed | tf_op | source)
XLA Modules:
  0.0 675.9 jit_solution(10893559086863316624)
XLA Ops:
  8.1 3.5 all_gather.3
  12.1 6.0 copy.12
  18.1 6.4 fusion.172
  27.9 3.4 stack.12
  31.3 11.4 %all-to-all-start = ((bf16[64,192,256]{2,1,0:T(8,128)(2,1)}), bf16[64,192,256]{2,1,0:T(8,128)(2,1)}, u32[]{:S(2)}, u32[]{:S(2)}) async-start(bf16[64,192,256]{2,1,0:T(8,128)(2,1)} %stack.12), calls=%async_computation | async-start | bytes 12582912 | tf_op jit(solution)/shard_map/all_to_all | solution.py:65
  42.8 79.3 %all-to-all-done = bf16[64,192,256]{2,1,0:T(8,128)(2,1)} async-done(((bf16[64,192,256]{2,1,0:T(8,128)(2,1)}), bf16[64,192,256]{2,1,0:T(8,128)(2,1)}, u32[]{:S(2)}, u32[]{:S(2)}) %all-to-all-start) | async-done | bytes 6291488 | tf_op jit(solution)/shard_map/all_to_all | solution.py:65
  125.4 8.3 %all-to-all-start.2 = ((bf16[64,192,256]{2,1,0:T(8,128)(2,1)}), bf16[64,192,256]{2,1,0:T(8,128)(2,1)}, u32[]{:S(2)}, u32[]{:S(2)}) async-start(bf16[64,192,256]{2,1,0:T(8,128)(2,1)} %stack.14), calls=%async_computation.2 | async-start | bytes 12582912 | tf_op jit(solution)/shard_map/all_to_all | solution.py:65
  133.8 79.9 %all-to-all-done.2 = bf16[64,192,256]{2,1,0:T(8,128)(2,1)} async-done(((bf16[64,192,256]{2,1,0:T(8,128)(2,1)}), bf16[64,192,256]{2,1,0:T(8,128)(2,1)}, u32[]{:S(2)}, u32[]{:S(2)}) %all-to-all-start.2) | async-done | bytes 6291488 | tf_op jit(solution)/shard_map/all_to_all | solution.py:65
  217.1 10.6 %all-to-all-start.3 = ((bf16[64,192,256]{2,1,0:T(8,128)(2,1)}), bf16[64,192,256]{2,1,0:T(8,128)(2,1)}, u32[]{:S(2)}, u32[]{:S(2)}) async-start(bf16[64,192,256]{2,1,0:T(8,128)(2,1)} %stack.15), calls=%async_computation.3 | async-start | bytes 12582912 | tf_op jit(solution)/shard_map/all_to_all | solution.py:65
  227.7 73.3 %all-to-all-done.3 = bf16[64,192,256]{2,1,0:T(8,128)(2,1)} async-done(((bf16[64,192,256]{2,1,0:T(8,128)(2,1)}), bf16[64,192,256]{2,1,0:T(8,128)(2,1)}, u32[]{:S(2)}, u32[]{:S(2)}) %all-to-all-start.3) | async-done | bytes 6291488 | tf_op jit(solution)/shard_map/all_to_all | solution.py:65
  301.0 3.4 stack.17
  304.4 12.8 %all-to-all-start.5 = ((bf16[64,192,256]{2,1,0:T(8,128)(2,1)}), bf16[64,192,256]{2,1,0:T(8,128)(2,1)}, u32[]{:S(2)}, u32[]{:S(2)}) async-start(bf16[64,192,256]{2,1,0:T(8,128)(2,1)} %stack.17), calls=%async_computation.5 | async-start | bytes 12582912 | tf_op jit(solution)/shard_map/all_to_all | solution.py:65
  317.2 73.5 %all-to-all-done.5 = bf16[64,192,256]{2,1,0:T(8,128)(2,1)} async-done(((bf16[64,192,256]{2,1,0:T(8,128)(2,1)}), bf16[64,192,256]{2,1,0:T(8,128)(2,1)}, u32[]{:S(2)}, u32[]{:S(2)}) %all-to-all-start.5) | async-done | bytes 6291488 | tf_op jit(solution)/shard_map/all_to_all | solution.py:65
  390.7 3.4 stack.16
  394.1 13.6 %all-to-all-start.4 = ((bf16[64,192,256]{2,1,0:T(8,128)(2,1)}), bf16[64,192,256]{2,1,0:T(8,128)(2,1)}, u32[]{:S(2)}, u32[]{:S(2)}) async-start(bf16[64,192,256]{2,1,0:T(8,128)(2,1)} %stack.16), calls=%async_computation.4 | async-start | bytes 12582912 | tf_op jit(solution)/shard_map/all_to_all | solution.py:65
  407.7 72.1 %all-to-all-done.4 = bf16[64,192,256]{2,1,0:T(8,128)(2,1)} async-done(((bf16[64,192,256]{2,1,0:T(8,128)(2,1)}), bf16[64,192,256]{2,1,0:T(8,128)(2,1)}, u32[]{:S(2)}, u32[]{:S(2)}) %all-to-all-start.4) | async-done | bytes 6291488 | tf_op jit(solution)/shard_map/all_to_all | solution.py:65
  483.3 13.5 %all-to-all-start.1 = ((bf16[64,192,256]{2,1,0:T(8,128)(2,1)}), bf16[64,192,256]{2,1,0:T(8,128)(2,1)}, u32[]{:S(2)}, u32[]{:S(2)}) async-start(bf16[64,192,256]{2,1,0:T(8,128)(2,1)} %stack.13), calls=%async_computation.1 | async-start | bytes 12582912 | tf_op jit(solution)/shard_map/all_to_all | solution.py:65
  499.5 6.9 %convolution_multiply_fusion.1 = f32[192,12288]{1,0:T(8,128)} fusion(bf16[12288,256]{1,0:T(8,128)(2,1)} %bitcast.11, bf16[192,768]{1,0:T(8,128)(2,1)S(1)} %convolution_convert_fusion.3), kind=kOutput, calls=%fused_computation.1 | convolution fusion | flops 606339072 | bytes 12632064 | tf_op jit(solution)/shard_map/dot_general | solution.py:69
  506.4 7.0 %convolution_multiply_fusion.2 = f32[192,12288]{1,0:T(8,128)} fusion(bf16[12288,256]{1,0:T(8,128)(2,1)} %bitcast.10, bf16[192,768]{1,0:T(8,128)(2,1)S(1)} %convolution_convert_fusion.3), kind=kOutput, calls=%fused_computation.2 | convolution fusion | flops 606339072 | bytes 12632064 | tf_op jit(solution)/shard_map/dot_general | solution.py:69
  513.5 6.9 %convolution_multiply_fusion.3 = f32[192,12288]{1,0:T(8,128)} fusion(bf16[12288,256]{1,0:T(8,128)(2,1)} %bitcast.9, bf16[192,768]{1,0:T(8,128)(2,1)S(1)} %convolution_convert_fusion.3), kind=kOutput, calls=%fused_computation.3 | convolution fusion | flops 606339072 | bytes 12632064 | tf_op jit(solution)/shard_map/dot_general | solution.py:69
  523.7 3.5 copy-done.1
  527.2 10.8 %select_reduce_fusion = (f32[192]{0:T(256)S(1)}, f32[192]{0:T(256)S(1)}, f32[192,12288]{1,0:T(8,128)}) fusion(s32[192]{0:T(256)S(1)} %get-tuple-element.17, s32[192]{0:T(256)S(1)} %get-tuple-element.16, f32[192,12288]{1,0:T(8,128)S(1)} %convolution_multiply_fusion.5, bf16[12288,256]{1,0:T(8,128)(2,1)} %bitcast.12, ...), kind=kOutput, calls=%fused_computation.7 | convolution fusion | flops 622853760 | bytes 22072832 | tf_op jit(solution)/shard_map/dot_general | solution.py:69
  537.9 30.9 %all-to-all-done.1 = bf16[64,192,256]{2,1,0:T(8,128)(2,1)} async-done(((bf16[64,192,256]{2,1,0:T(8,128)(2,1)}), bf16[64,192,256]{2,1,0:T(8,128)(2,1)}, u32[]{:S(2)}, u32[]{:S(2)}) %all-to-all-start.1) | async-done | bytes 6291488 | tf_op jit(solution)/shard_map/all_to_all | solution.py:65
  568.8 22.5 %fusion.11 = (f32[192]{0:T(256)S(1)}, f32[192]{0:T(256)S(1)}, f32[192]{0:T(256)S(1)}, f32[192]{0:T(256)S(1)}, f32[192]{0:T(256)S(1)}, /*index=5*/f32[192]{0:T(256)S(1)}, f32[192,12288]{1,0:T(8,128)}) fusion(f32[192,12288]{1,0:T(8,128)} %get-tuple-element.33, f32[192]{0:T(256)S(1)} %get-tuple-element.10, s32[192]{0:T(256)S(1)} %get-tuple-element.17, ...), kind=kOutput, calls=%fused_computation.31 | convolution fusion | flops 646445952 | bytes 59826688 | tf_op jit(solution)/shard_map/dot_general | solution.py:69
  591.4 7.7 %fusion.65 = bf16[192,768]{1,0:T(8,128)(2,1)S(1)} fusion(bf16[12288,256]{1,0:T(8,128)(2,1)} %bitcast.7, f32[192,12288]{1,0:T(8,128)} %copy-done.1, f32[192]{0:T(256)S(1)} %get-tuple-element.11, f32[192]{0:T(256)S(1)} %get-tuple-element.9, s32[192]{0:T(256)S(1)} %get-tuple-element.17, s32[192]{0:T(256)S(1)} %get-tuple-element.16), kind=kOutput, calls=%fused_computation.77 | convolution fusion | flops 618184704 | bytes 12635136 | tf_op jit(solution)/shard_map/dot_general | solution.py:75
  601.3 12.1 %fusion.9 = (f32[192]{0:T(256)S(1)}, f32[192]{0:T(256)S(1)}, f32[192]{0:T(256)S(1)}, f32[192]{0:T(256)S(1)}) fusion(f32[192,12288]{1,0:T(8,128)S(1)} %bitcast.25, f32[192]{0:T(256)S(1)} %get-tuple-element.8, s32[192]{0:T(256)S(1)} %get-tuple-element.17, s32[192]{0:T(256)S(1)} %get-tuple-element.16, f32[192,12288]{1,0:T(8,128)} %get-tuple-element.34, ...), kind=kLoop, calls=%fused_computation.29 | loop fusion | flops 35388672 | bytes 37756416 | tf_op jit(solution)/shard_map/reduce_sum | solution.py:74
  613.4 7.6 %fusion.80 = bf16[192,768]{1,0:T(8,128)(2,1)S(1)} fusion(bf16[192,768]{1,0:T(8,128)(2,1)S(1)} %fusion.65, bf16[12288,256]{1,0:T(8,128)(2,1)} %bitcast.8, f32[192,12288]{1,0:T(8,128)} %get-tuple-element.34, f32[192]{0:T(256)S(1)} %get-tuple-element.5, f32[192]{0:T(256)S(1)} %get-tuple-element.13, s32[192]{0:T(256)S(1)} %get-tuple-element.17, ...), kind=kOutput, calls=%fused_computation.80 | convolution fusion | flops 618184704 | bytes 12636160 | tf_op jit(solution)/shard_map/dot_general | solution.py:75
  621.0 7.7 %fusion.95 = bf16[192,768]{1,0:T(8,128)(2,1)S(1)} fusion(bf16[192,768]{1,0:T(8,128)(2,1)S(1)} %fusion.80, bf16[12288,256]{1,0:T(8,128)(2,1)} %bitcast.9, f32[192,12288]{1,0:T(8,128)} %convolution_multiply_fusion.3, f32[192]{0:T(256)S(1)} %get-tuple-element.6, f32[192]{0:T(256)S(1)} %get-tuple-element.14, s32[192]{0:T(256)S(1)} %get-tuple-element.17, ...), kind=kOutput, calls=%fused_computation.83 | convolution fusion | flops 618184704 | bytes 12636160 | tf_op jit(solution)/shard_map/dot_general | solution.py:75
  628.7 4.9 fusion.110
  633.6 5.1 fusion.125
  638.7 7.7 %fusion.140 = bf16[192,768]{1,0:T(8,128)(2,1)S(1)} fusion(bf16[192,768]{1,0:T(8,128)(2,1)S(1)} %fusion.125, bf16[12288,256]{1,0:T(8,128)(2,1)} %bitcast.12, f32[192,12288]{1,0:T(8,128)} %get-tuple-element.33, f32[192]{0:T(256)S(1)} %get-tuple-element.10, f32[192]{0:T(256)S(1)} %get-tuple-element.4, s32[192]{0:T(256)S(1)} %get-tuple-element.17, ...), kind=kOutput, calls=%fused_computation.92 | convolution fusion | flops 618184704 | bytes 12636160 | tf_op jit(solution)/shard_map/dot_general | solution.py:75
  647.9 19.1 %reduce-scatter.2.cloned.1.call-done = bf16[192,768]{1,0:T(8,128)(2,1)} async-done(((bf16[192,1536]{1,0:T(8,128)(2,1)}), bf16[192,768]{1,0:T(8,128)(2,1)}) %reduce-scatter.2.cloned.1.call-update) | async-done | bytes 294928 | tf_op jit(solution)/shard_map/reduce_scatter | solution.py:81
  (69 shorter events, 25.6 us)
Async XLA Ops:
  7.2 639.2 %copy-start = (bf16[768,1536]{1,0:T(8,128)(2,1)S(1)}, bf16[768,1536]{1,0:T(8,128)(2,1)}, u32[]{:S(2)}) copy-start(bf16[768,1536]{1,0:T(8,128)(2,1)} %param.17) | copy-start | bytes 7077892
  11.7 15.2 %copy-start.6 = (f32[192]{0:T(256)}, f32[192]{0:T(256)S(1)}, u32[]{:S(2)}) copy-start(f32[192]{0:T(256)S(1)} %broadcast_multiply_fusion) | copy-start | bytes 2308
  12.0 14.9 %copy-start.8 = (f32[192]{0:T(256)}, f32[192]{0:T(256)S(1)}, u32[]{:S(2)}) copy-start(f32[192]{0:T(256)S(1)} %add_rsqrt_fusion) | copy-start | bytes 2308
  12.1 12.4 %copy-start.3 = (f32[3,1536]{1,0:T(4,128)S(1)}, f32[3,1536]{1,0:T(4,128)}, u32[]{:S(2)}) copy-start(f32[3,1536]{1,0:T(4,128)} %param.13) | copy-start | bytes 55300
  18.1 8.9 %copy-start.10 = (bf16[1536,768]{1,0:T(8,128)(2,1)S(1)}, bf16[1536,768]{1,0:T(8,128)(2,1)}, u32[]{:S(2)}) copy-start(bf16[1536,768]{1,0:T(8,128)(2,1)} %param.16) | copy-start | bytes 7077892
  24.6 2.4 copy-start.4
  31.3 90.7 %all-to-all-start = ((bf16[64,192,256]{2,1,0:T(8,128)(2,1)}), bf16[64,192,256]{2,1,0:T(8,128)(2,1)}, u32[]{:S(2)}, u32[]{:S(2)}) async-start(bf16[64,192,256]{2,1,0:T(8,128)(2,1)} %stack.12), calls=%async_computation | async-start | bytes 12582912 | tf_op jit(solution)/shard_map/all_to_all | solution.py:65
  125.4 88.3 %all-to-all-start.2 = ((bf16[64,192,256]{2,1,0:T(8,128)(2,1)}), bf16[64,192,256]{2,1,0:T(8,128)(2,1)}, u32[]{:S(2)}, u32[]{:S(2)}) async-start(bf16[64,192,256]{2,1,0:T(8,128)(2,1)} %stack.14), calls=%async_computation.2 | async-start | bytes 12582912 | tf_op jit(solution)/shard_map/all_to_all | solution.py:65
  217.1 83.9 %all-to-all-start.3 = ((bf16[64,192,256]{2,1,0:T(8,128)(2,1)}), bf16[64,192,256]{2,1,0:T(8,128)(2,1)}, u32[]{:S(2)}, u32[]{:S(2)}) async-start(bf16[64,192,256]{2,1,0:T(8,128)(2,1)} %stack.15), calls=%async_computation.3 | async-start | bytes 12582912 | tf_op jit(solution)/shard_map/all_to_all | solution.py:65
  304.4 86.3 %all-to-all-start.5 = ((bf16[64,192,256]{2,1,0:T(8,128)(2,1)}), bf16[64,192,256]{2,1,0:T(8,128)(2,1)}, u32[]{:S(2)}, u32[]{:S(2)}) async-start(bf16[64,192,256]{2,1,0:T(8,128)(2,1)} %stack.17), calls=%async_computation.5 | async-start | bytes 12582912 | tf_op jit(solution)/shard_map/all_to_all | solution.py:65
  394.1 85.7 %all-to-all-start.4 = ((bf16[64,192,256]{2,1,0:T(8,128)(2,1)}), bf16[64,192,256]{2,1,0:T(8,128)(2,1)}, u32[]{:S(2)}, u32[]{:S(2)}) async-start(bf16[64,192,256]{2,1,0:T(8,128)(2,1)} %stack.16), calls=%async_computation.4 | async-start | bytes 12582912 | tf_op jit(solution)/shard_map/all_to_all | solution.py:65
  483.3 13.6 %copy-start.11 = (s32[5]{0:T(128)S(1)}, s32[5]{0:T(128)}, u32[]{:S(2)}) copy-start(s32[5]{0:T(128)} %param.10) | copy-start | bytes 64
  483.3 13.8 %copy-start.5 = (f32[1536]{0:T(1024)S(1)}, f32[1536]{0:T(1024)}, u32[]{:S(2)}) copy-start(f32[1536]{0:T(1024)} %copy-done.4) | copy-start | bytes 18436
  483.3 13.8 %copy-start.7 = (f32[192]{0:T(256)S(1)}, f32[192]{0:T(256)}, u32[]{:S(2)}) copy-start(f32[192]{0:T(256)} %copy-done.6) | copy-start | bytes 2308
  483.3 13.9 %copy-start.9 = (f32[192]{0:T(256)S(1)}, f32[192]{0:T(256)}, u32[]{:S(2)}) copy-start(f32[192]{0:T(256)} %copy-done.8) | copy-start | bytes 2308
  483.3 85.5 %all-to-all-start.1 = ((bf16[64,192,256]{2,1,0:T(8,128)(2,1)}), bf16[64,192,256]{2,1,0:T(8,128)(2,1)}, u32[]{:S(2)}, u32[]{:S(2)}) async-start(bf16[64,192,256]{2,1,0:T(8,128)(2,1)} %stack.13), calls=%async_computation.1 | async-start | bytes 12582912 | tf_op jit(solution)/shard_map/all_to_all | solution.py:65
  496.8 170.2 %reduce-scatter.2.cloned.1.call-start = ((), (), s32[]{:S(2)}) async-start(), calls=%async_computation.7 | async-start | bytes 884736 | tf_op jit(solution)/shard_map/reduce_scatter | solution.py:81
  523.7 3.5 copy-start.1
  591.3 7.8 %slice-start = ((s8[9437184]{0:T(1024)(128)(4,1)}), s8[4194304]{0:T(1024)(128)(4,1)S(1)}, s32[]{:S(2)}) async-start(s8[9437184]{0:T(1024)(128)(4,1)} %bitcast.24), calls=%async_computation.8 | async-start | bytes 8388608
  591.3 7.8 %slice-start.3 = ((s8[9437184]{0:T(1024)(128)(4,1)}), s8[4194304]{0:T(1024)(128)(4,1)S(1)}, s32[]{:S(2)}) async-start(s8[9437184]{0:T(1024)(128)(4,1)} %bitcast.26), calls=%async_computation.11 | async-start | bytes 8388608
  591.4 8.2 %slice-start.1 = ((s8[9437184]{0:T(1024)(128)(4,1)}), s8[4194304]{0:T(1024)(128)(4,1)S(1)}, s32[]{:S(2)}) async-start(s8[9437184]{0:T(1024)(128)(4,1)} %bitcast.24), calls=%async_computation.9 | async-start | bytes 8388608
  591.4 8.4 %slice-start.2 = ((s8[9437184]{0:T(1024)(128)(4,1)}), s8[1048576]{0:T(1024)(128)(4,1)S(1)}, s32[]{:S(2)}) async-start(s8[9437184]{0:T(1024)(128)(4,1)} %bitcast.24), calls=%async_computation.10 | async-start | bytes 2097152
  591.4 9.7 %slice-start.4 = ((s8[9437184]{0:T(1024)(128)(4,1)}), s8[4194304]{0:T(1024)(128)(4,1)S(1)}, s32[]{:S(2)}) async-start(s8[9437184]{0:T(1024)(128)(4,1)} %bitcast.26), calls=%async_computation.12 | async-start | bytes 8388608
  591.4 9.9 %slice-start.5 = ((s8[9437184]{0:T(1024)(128)(4,1)}), s8[1048576]{0:T(1024)(128)(4,1)S(1)}, s32[]{:S(2)}) async-start(s8[9437184]{0:T(1024)(128)(4,1)} %bitcast.26), calls=%async_computation.13 | async-start | bytes 2097152
  638.7 28.3 %copy-start.2 = (bf16[192,768]{1,0:T(8,128)(2,1)S(1)}, bf16[192,768]{1,0:T(8,128)(2,1)}, u32[]{:S(2)}) copy-start(bf16[192,768]{1,0:T(8,128)(2,1)} %param.9) | copy-start | bytes 884740
Sparse Core Ops, SparseCore 0:
  648.0 19.0 reduce-scatter.1
